TPU v7x, 256 devices: a whole 4x4x8 slice. The times are simulated.
256 devices in a mesh: row: 32 (over y_lo, z, core), col: 8 (over y_hi, x).
Axes of the slice: x: 4, y: 4 (y_hi: 2, y_lo: 2; y = y_hi * 2 + y_lo), z: 8, core: 2. Of those that a mesh axis runs over, the one named last changes fastest.
Arguments:
- features: bfloat16 [262144, 256], P(('row', 'col')), may hold values from -6 to 6
- tile_values: bfloat16 [32, 8, 256, 128, 128], P('row', 'col'), may hold values from -0.09375 to 0.09375
- tile_rows: int32 [32, 8, 256], P('row', 'col'), may hold values from 0 to 63
- tile_cols: int32 [32, 8, 256], P('row', 'col'), may hold values from 0 to 255
- tile_count: int32 [32, 8], P('row', 'col'), may hold values from 64 to 256, as said below
- weight: bfloat16 [256, 256], replicated, may hold values from -0.375 to 0.375
Outputs:
- layer_out: bfloat16 [262144, 256], P(('row', 'col'))
Inputs may be any that keep to these rules, and one draw needn't show every extreme that they name: `tile_count`: live slots of one row block and column group; some block is full in every draw.
All inputs are finite; a program needn't handle non-finite values.
Results may differ from a plain program's by a relative error of at most 0.015.
Values may be sent and summed in bfloat16 or wider, within the bound.
A program may use at most 128 MiB of HBM per device.

v0:
```python
import math
import jax
import jax.numpy as jnp
from jax import lax
from jax.sharding import PartitionSpec as P


def local(features, tile_values, tile_rows, tile_cols, tile_count, weight):
    slab_rows, width = features.shape
    tiles = tile_values.shape[2]
    side = tile_values.shape[3]
    values = tile_values.reshape(tiles, side, side)
    rows_idx = tile_rows.reshape(tiles)
    cols_idx = tile_cols.reshape(tiles)
    count = tile_count.reshape(())
    group = lax.all_gather(features, "row", axis=0, tiled=True)
    col_count = group.shape[0] // side
    col_tiles = group.reshape(col_count, side, width)
    n_cols = lax.axis_size("col")
    row_tiles = n_cols * slab_rows // side
    block_len = math.gcd(tiles, 64)

    def accumulate(turn, carry):
        start = turn * block_len
        vals = lax.dynamic_slice_in_dim(values, start, block_len, 0)
        picks = lax.dynamic_slice_in_dim(cols_idx, start, block_len, 0)
        targets = lax.dynamic_slice_in_dim(rows_idx, start, block_len, 0)
        inputs = jnp.take(col_tiles, picks, axis=0)
        products = jnp.einsum("kij,kjf->kif", vals, inputs, preferred_element_type=jnp.float32)
        live = (start + jnp.arange(block_len, dtype=jnp.int32) < count).astype(jnp.float32)
        products = products * live[:, None, None]
        return carry.at[targets].add(products)

    carry = lax.fori_loop(
        0, tiles // block_len, accumulate, jnp.zeros((row_tiles, side, width), jnp.float32)
    )
    rounded = lax.optimization_barrier(carry.reshape(row_tiles * side, width).astype(jnp.bfloat16))
    partial_value = rounded.astype(jnp.float32)
    total = lax.psum(partial_value.astype(jnp.bfloat16), "col").astype(jnp.float32)
    summed = lax.dynamic_slice_in_dim(total, lax.axis_index("col") * slab_rows, slab_rows, 0)
    aggregated = summed.astype(jnp.bfloat16)
    return jnp.dot(aggregated, weight, preferred_element_type=jnp.float32).astype(jnp.bfloat16)


def solution(mesh):
    return jax.shard_map(
        local,
        mesh=mesh,
        in_specs=(
            P(("row", "col"), None),
            P("row", "col", None, None, None),
            P("row", "col", None),
            P("row", "col", None),
            P("row", "col"),
            P(),
        ),
        out_specs=P(("row", "col"), None),
        check_vma=False,
    )
```

profile of v0, /device:TPU:1, one launch (start us, length us, event | category | flops | bytes accessed | tf_op | source)
XLA Modules:
  0.0 392.6 jit_solution(11642625156492963269)
XLA Ops:
  6.5 0.0 copy-start
  6.5 0.0 copy-start.2
  6.5 0.0 copy-start.1
  6.5 0.0 all-gather.2.cloned.1.call-start
  6.5 0.7 all-gather.2.cloned.1.call-update
  7.3 0.0 all-reduce.2.cloned.1.call-start
  7.3 105.8 %all-gather.2.cloned.1.call-done = bf16[32768,256]{1,0:T(8,128)(2,1)} async-done(((bf16[1024,256]{1,0:T(8,128)(2,1)}), bf16[32768,256]{1,0:T(8,128)(2,1)}) %all-gather.2.cloned.1.call-update) | async-done | bytes 16777232 | tf_op jit(solution)/shard_map/all_gather | solution.py:16
  113.1 4.2 %broadcast_in_dim.37 = f32[64,128,256]{2,1,0:T(8,128)} broadcast(f32[]{:T(128)} %constant.62.clone.1), dimensions={} | broadcast | bytes 8388612 | tf_op jit(solution)/shard_map/broadcast_in_dim | solution.py:35
  117.3 0.0 copy-done.2
  117.4 0.0 copy-done.1
  117.4 145.0 %while.13 = (s32[]{:T(128)}, f32[64,128,256]{2,1,0:T(8,128)}, s32[256]{0:T(256)S(1)}, bf16[256,128,128]{2,1,0:T(8,128)(2,1)}, s32[256]{0:T(256)S(1)}, /*index=5*...) while((s32[]{:T(128)}, f32[64,128,256]{2,1,0:T(8,128)}, ...), condition=%wide.region_2.3_spmd, body=%wide.region_0.2_spmd.sunk | while | flops 543164160 | bytes 48241208 | solution.py:34
  117.4 0.1 compare_select_fusion.4
  117.4 0.7 compare_and_fusion.2
  118.2 8.6 %gather_fusion = bf16[64,128,256]{2,1,0:T(8,128)(2,1)} fusion(bf16[256,128,256]{2,1,0:T(8,128)(2,1)} %get-tuple-element.223, s32[1024]{0:T(1024)S(1)} %pad_clamp_fusion.2), kind=kCustom, calls=%fused_computation.clone.1 | custom fusion | bytes 8388864 | tf_op jit(solution)/shard_map/while/body/eval_jaxpr/jit(_take)/gather | solution.py:28
  126.8 7.4 %broadcast_multiply_fusion.2 = f32[64,128,256]{2,1,0:T(8,128)} fusion(f32[64]{0:T(128)S(1)} %get-tuple-element.193, bf16[64,128,256]{2,1,0:T(8,128)(2,1)} %gather_fusion, pred[64]{0:T(512)(128)(4,1)S(1)} %get-tuple-element.195, bf16[256,128,128]{2,1,0:T(8,128)(2,1)} %get-tuple-element.221, s32[]{:T(128)S(6)} %select_n.49), kind=kOutput, calls=%fused_computation.2.clone.1 | convolution fusion | flops 541065216 | bytes 14680388 | tf_op jit(solution)/shard_map/while/body/eval_jaxpr/kij,kjf->kif/dot_general | solution.py:29
  134.2 19.4 %scatter_fusion = f32[64,128,256]{2,1,0:T(8,128)} fusion(f32[64,128,256]{2,1,0:T(8,128)} %get-tuple-element.208, s32[64]{0:T(128)S(1)} %compare_select_fusion.4, f32[64,128,256]{2,1,0:T(8,128)} %broadcast_multiply_fusion.2), kind=kCustom, calls=%fused_computation.1.clone.1 | custom fusion | flops 2097152 | bytes 25166080 | tf_op jit(solution)/shard_map/while/body/eval_jaxpr/scatter-add | solution.py:32
  153.5 0.1 compare_select_fusion.4
  153.6 0.7 compare_and_fusion.2
  154.3 8.6 %gather_fusion = bf16[64,128,256]{2,1,0:T(8,128)(2,1)} fusion(bf16[256,128,256]{2,1,0:T(8,128)(2,1)} %get-tuple-element.223, s32[1024]{0:T(1024)S(1)} %pad_clamp_fusion.2), kind=kCustom, calls=%fused_computation.clone.1 | custom fusion | bytes 8388864 | tf_op jit(solution)/shard_map/while/body/eval_jaxpr/jit(_take)/gather | solution.py:28
  163.0 7.4 %broadcast_multiply_fusion.2 = f32[64,128,256]{2,1,0:T(8,128)} fusion(f32[64]{0:T(128)S(1)} %get-tuple-element.193, bf16[64,128,256]{2,1,0:T(8,128)(2,1)} %gather_fusion, pred[64]{0:T(512)(128)(4,1)S(1)} %get-tuple-element.195, bf16[256,128,128]{2,1,0:T(8,128)(2,1)} %get-tuple-element.221, s32[]{:T(128)S(6)} %select_n.49), kind=kOutput, calls=%fused_computation.2.clone.1 | convolution fusion | flops 541065216 | bytes 14680388 | tf_op jit(solution)/shard_map/while/body/eval_jaxpr/kij,kjf->kif/dot_general | solution.py:29
  170.4 19.4 %scatter_fusion = f32[64,128,256]{2,1,0:T(8,128)} fusion(f32[64,128,256]{2,1,0:T(8,128)} %get-tuple-element.208, s32[64]{0:T(128)S(1)} %compare_select_fusion.4, f32[64,128,256]{2,1,0:T(8,128)} %broadcast_multiply_fusion.2), kind=kCustom, calls=%fused_computation.1.clone.1 | custom fusion | flops 2097152 | bytes 25166080 | tf_op jit(solution)/shard_map/while/body/eval_jaxpr/scatter-add | solution.py:32
  189.8 0.1 compare_select_fusion.4
  189.9 0.7 compare_and_fusion.2
  190.6 8.6 %gather_fusion = bf16[64,128,256]{2,1,0:T(8,128)(2,1)} fusion(bf16[256,128,256]{2,1,0:T(8,128)(2,1)} %get-tuple-element.223, s32[1024]{0:T(1024)S(1)} %pad_clamp_fusion.2), kind=kCustom, calls=%fused_computation.clone.1 | custom fusion | bytes 8388864 | tf_op jit(solution)/shard_map/while/body/eval_jaxpr/jit(_take)/gather | solution.py:28
  199.2 7.4 %broadcast_multiply_fusion.2 = f32[64,128,256]{2,1,0:T(8,128)} fusion(f32[64]{0:T(128)S(1)} %get-tuple-element.193, bf16[64,128,256]{2,1,0:T(8,128)(2,1)} %gather_fusion, pred[64]{0:T(512)(128)(4,1)S(1)} %get-tuple-element.195, bf16[256,128,128]{2,1,0:T(8,128)(2,1)} %get-tuple-element.221, s32[]{:T(128)S(6)} %select_n.49), kind=kOutput, calls=%fused_computation.2.clone.1 | convolution fusion | flops 541065216 | bytes 14680388 | tf_op jit(solution)/shard_map/while/body/eval_jaxpr/kij,kjf->kif/dot_general | solution.py:29
  206.6 19.4 %scatter_fusion = f32[64,128,256]{2,1,0:T(8,128)} fusion(f32[64,128,256]{2,1,0:T(8,128)} %get-tuple-element.208, s32[64]{0:T(128)S(1)} %compare_select_fusion.4, f32[64,128,256]{2,1,0:T(8,128)} %broadcast_multiply_fusion.2), kind=kCustom, calls=%fused_computation.1.clone.1 | custom fusion | flops 2097152 | bytes 25166080 | tf_op jit(solution)/shard_map/while/body/eval_jaxpr/scatter-add | solution.py:32
  226.0 0.1 compare_select_fusion.4
  226.1 0.7 compare_and_fusion.2
  226.9 8.6 %gather_fusion = bf16[64,128,256]{2,1,0:T(8,128)(2,1)} fusion(bf16[256,128,256]{2,1,0:T(8,128)(2,1)} %get-tuple-element.223, s32[1024]{0:T(1024)S(1)} %pad_clamp_fusion.2), kind=kCustom, calls=%fused_computation.clone.1 | custom fusion | bytes 8388864 | tf_op jit(solution)/shard_map/while/body/eval_jaxpr/jit(_take)/gather | solution.py:28
  235.5 7.4 %broadcast_multiply_fusion.2 = f32[64,128,256]{2,1,0:T(8,128)} fusion(f32[64]{0:T(128)S(1)} %get-tuple-element.193, bf16[64,128,256]{2,1,0:T(8,128)(2,1)} %gather_fusion, pred[64]{0:T(512)(128)(4,1)S(1)} %get-tuple-element.195, bf16[256,128,128]{2,1,0:T(8,128)(2,1)} %get-tuple-element.221, s32[]{:T(128)S(6)} %select_n.49), kind=kOutput, calls=%fused_computation.2.clone.1 | convolution fusion | flops 541065216 | bytes 14680388 | tf_op jit(solution)/shard_map/while/body/eval_jaxpr/kij,kjf->kif/dot_general | solution.py:29
  242.9 19.5 %scatter_fusion = f32[64,128,256]{2,1,0:T(8,128)} fusion(f32[64,128,256]{2,1,0:T(8,128)} %get-tuple-element.208, s32[64]{0:T(128)S(1)} %compare_select_fusion.4, f32[64,128,256]{2,1,0:T(8,128)} %broadcast_multiply_fusion.2), kind=kCustom, calls=%fused_computation.1.clone.1 | custom fusion | flops 2097152 | bytes 25166080 | tf_op jit(solution)/shard_map/while/body/eval_jaxpr/scatter-add | solution.py:32
  262.4 5.9 %convert_element_type.28 = bf16[64,128,256]{2,1,0:T(8,128)(2,1)} convert(f32[64,128,256]{2,1,0:T(8,128)} %get-tuple-element.129) | non-fusion elementwise | flops 2097152 | bytes 12582912 | tf_op jit(solution)/shard_map/convert_element_type | solution.py:37
  268.3 0.0 all-reduce.2.cloned.1.call-update
  268.4 115.3 %all-reduce.2.cloned.1.call-done = bf16[8192,256]{1,0:T(8,128)(2,1)} async-done(((bf16[8192,256]{1,0:T(8,128)(2,1)}), bf16[8192,256]{1,0:T(8,128)(2,1)}) %all-reduce.2.cloned.1.call-update) | async-done | bytes 4194320 | tf_op jit(solution)/shard_map/psum | solution.py:39
  383.7 0.0 copy-done
  383.7 2.1 convolution_convert_fusion
  (4 shorter events, 0.0 us)
Async XLA Ops:
  6.5 377.1 %copy-start = (bf16[256,256]{1,0:T(8,128)(2,1)S(1)}, bf16[256,256]{1,0:T(8,128)(2,1)}, u32[]{:S(2)}) copy-start(bf16[256,256]{1,0:T(8,128)(2,1)} %param.13) | copy-start | bytes 393220
  6.5 110.8 %copy-start.2 = (s32[1,1,256]{2,1,0:T(1,128)S(1)}, s32[1,1,256]{2,1,0:T(1,128)}, u32[]{:S(2)}) copy-start(s32[1,1,256]{2,1,0:T(1,128)} %param.10) | copy-start | bytes 3076
  6.5 110.8 %copy-start.1 = (s32[1,1,256]{2,1,0:T(1,128)S(1)}, s32[1,1,256]{2,1,0:T(1,128)}, u32[]{:S(2)}) copy-start(s32[1,1,256]{2,1,0:T(1,128)} %param.11) | copy-start | bytes 3076
  6.5 106.6 %all-gather.2.cloned.1.call-start = ((), (), s32[]{:S(2)}) async-start(), calls=%async_computation | async-start | bytes 17301504 | tf_op jit(solution)/shard_map/all_gather | solution.py:16
  7.3 376.4 %all-reduce.2.cloned.1.call-start = ((), (), s32[]{:S(2)}) async-start(), calls=%async_computation.1 | async-start | bytes 8388608 | tf_op jit(solution)/shard_map/psum | solution.py:39
Sparse Core Ops, SparseCore 0:
  9.2 103.8 all-gather.1
  268.5 115.1 all-reduce.1
where the time goes:
time: 393 us
  waiting for transfers between devices  222 us (56%)
  other arithmetic  86.9 us (22%)
  local copies, waits for them, and re-layouts  38.8 us (10%)
  matrix products  31.6 us (8%)
  between operations  13.4 us (3%)
    psum x1, waiting for transfers between devices, local(): lax.psum(partial_value.astype(jnp.bfloat16), 'col').astype(jnp.float32)  115 us
    all_gather x1, waiting for transfers between devices, local(): group = lax.all_gather(features, 'row', axis=0, tiled=True)  106 us
    scatter-add x4, other arithmetic, accumulate(): return carry.at[targets].add(products)  77.8 us
    gather x4, local copies, waits for them, and re-layouts, accumulate(): inputs = jnp.take(col_tiles, picks, axis=0)  34.5 us
    dot_general x4, matrix products, accumulate(): jnp.einsum('kij,kjf->kif', vals, inputs, preferred_element_type=jnp.float32)  29.5 us
  transfers between devices with their start and end apart: 2, of which 2 were waited for; matrix products, arithmetic and copies ran while one was open for 0% of the time, Pallas kernels for 0%

commit v1 on v0

--- a/solution.py
+++ b/solution.py
@@ -13,7 +13,9 @@
     rows_idx = tile_rows.reshape(tiles)
     cols_idx = tile_cols.reshape(tiles)
     count = tile_count.reshape(())
-    group = lax.all_gather(features, "row", axis=0, tiled=True)
+    group = jnp.concatenate(
+        lax.all_to_all(jnp.stack([features] * lax.axis_size("row")), "row", 0, 0), axis=0
+    )
     col_count = group.shape[0] // side
     col_tiles = group.reshape(col_count, side, width)
     n_cols = lax.axis_size("col")

time: 393 us -> 676 us (1.72)
  waiting for transfers between devices: 222 us -> 486 us
  starting transfers between devices: 0.04 us -> 11.2 us
  local copies, waits for them, and re-layouts: 38.8 us -> 45.6 us
    all_to_all x0 -> x1, waiting for transfers between devices: none -> 361 us  [local(): lax.all_to_all(jnp.stack([features] * lax.axis_size('row')), 'row', 0, 0)]
    all_gather x1 -> x0, waiting for transfers between devices: 106 us -> none  [local(): group = lax.all_gather(features, 'row', axis=0, tiled=True)]
    all_to_all x0 -> x1, starting transfers between devices: none -> 11.2 us  [local(): lax.all_to_all(jnp.stack([features] * lax.axis_size('row')), 'row', 0, 0)]
    psum x1, waiting for transfers between devices: 115 us -> 125 us  [local(): lax.psum(partial_value.astype(jnp.bfloat16), 'col').astype(jnp.float32)]
    another operation x0 -> x1, local copies, waits for them, and re-layouts: none -> 6.81 us  [local(): jnp.stack([features] * lax.axis_size('row'))]
where the time goes in v1:
time: 676 us; the launch traced here: 675 us
  waiting for transfers between devices  486 us (72%)
  other arithmetic  87.1 us (13%)
  local copies, waits for them, and re-layouts  45.6 us (7%)
  matrix products  31.6 us (5%)
  between operations  13.4 us (2%)
  starting transfers between devices  11.2 us (2%)
    all_to_all x1, waiting for transfers between devices, local(): lax.all_to_all(jnp.stack([features] * lax.axis_size('row')), 'row', 0, 0)  361 us
    psum x1, waiting for transfers between devices, local(): lax.psum(partial_value.astype(jnp.bfloat16), 'col').astype(jnp.float32)  125 us
    scatter-add x4, other arithmetic, accumulate(): return carry.at[targets].add(products)  77.9 us
    gather x4, local copies, waits for them, and re-layouts, accumulate(): inputs = jnp.take(col_tiles, picks, axis=0)  34.6 us
    dot_general x4, matrix products, accumulate(): jnp.einsum('kij,kjf->kif', vals, inputs, preferred_element_type=jnp.float32)  29.5 us
  transfers between devices with their start and end apart: 2, of which 2 were waited for; matrix products, arithmetic and copies ran while one was open for 0% of the time, Pallas kernels for 0%

profile of v1, /device:TPU:1, one launch (start us, length us, event | category | flops | bytes accessed | tf_op | source)
XLA Modules:
  0.0 675.2 jit_solution(9471773652205910320)
XLA Ops:
  6.5 0.0 copy-start
  6.5 6.8 %stack.2 = bf16[32,1024,256]{2,1,0:T(8,128)(2,1)} broadcast(bf16[1024,256]{1,0:T(8,128)(2,1)} %param.8), dimensions={1,2} | broadcast | bytes 17301504 | tf_op jit(solution)/shard_map/stack | solution.py:17
  13.3 11.2 %all-to-all-start = ((bf16[32,1024,256]{2,1,0:T(8,128)(2,1)}), bf16[32,1024,256]{2,1,0:T(8,128)(2,1)}, u32[]{:S(2)}, u32[]{:S(2)}) async-start(bf16[32,1024,256]{2,1,0:T(8,128)(2,1)} %stack.2), calls=%async_computation | async-start | bytes 33554432 | tf_op jit(solution)/shard_map/all_to_all | solution.py:17
  24.5 0.0 copy-start.1
  24.5 0.0 copy-start.2
  24.6 0.0 all-reduce.2.cloned.1.call-start
  24.6 361.1 %all-to-all-done = bf16[32,1024,256]{2,1,0:T(8,128)(2,1)} async-done(((bf16[32,1024,256]{2,1,0:T(8,128)(2,1)}), bf16[32,1024,256]{2,1,0:T(8,128)(2,1)}, u32[]{:S(2)}, u32[]{:S(2)}) %all-to-all-start) | async-done | bytes 16777248 | tf_op jit(solution)/shard_map/all_to_all | solution.py:17
  385.7 4.2 broadcast_in_dim.37
  390.0 0.0 copy-done.1
  390.0 0.0 copy-done.2
  390.0 145.2 %while.13 = (s32[]{:T(128)}, f32[64,128,256]{2,1,0:T(8,128)}, s32[256]{0:T(256)S(1)}, bf16[256,128,128]{2,1,0:T(8,128)(2,1)}, s32[256]{0:T(256)S(1)}, /*index=5*...) while((s32[]{:T(128)}, f32[64,128,256]{2,1,0:T(8,128)}, ...), condition=%wide.region_2.3_spmd, body=%wide.region_0.2_spmd.sunk | while | flops 543164160 | bytes 48241200 | solution.py:36
  390.0 0.7 compare_and_fusion.2
  390.7 8.6 %gather_fusion = bf16[64,128,256]{2,1,0:T(8,128)(2,1)} fusion(bf16[256,128,256]{2,1,0:T(8,128)(2,1)} %get-tuple-element.223, s32[1024]{0:T(1024)S(1)} %pad_clamp_fusion.2), kind=kCustom, calls=%fused_computation.clone.1 | custom fusion | bytes 8388864 | tf_op jit(solution)/shard_map/while/body/eval_jaxpr/jit(_take)/gather | solution.py:30
  399.3 7.4 %broadcast_multiply_fusion.2 = f32[64,128,256]{2,1,0:T(8,128)} fusion(f32[64]{0:T(128)S(1)} %get-tuple-element.193, bf16[64,128,256]{2,1,0:T(8,128)(2,1)} %gather_fusion, pred[64]{0:T(512)(128)(4,1)S(1)} %get-tuple-element.195, bf16[256,128,128]{2,1,0:T(8,128)(2,1)} %get-tuple-element.221, s32[]{:T(128)S(6)} %select_n.49), kind=kOutput, calls=%fused_computation.2.clone.1 | convolution fusion | flops 541065216 | bytes 14680388 | tf_op jit(solution)/shard_map/while/body/eval_jaxpr/kij,kjf->kif/dot_general | solution.py:31
  406.7 0.1 compare_select_fusion.4
  406.8 19.5 %scatter_fusion = f32[64,128,256]{2,1,0:T(8,128)} fusion(f32[64,128,256]{2,1,0:T(8,128)} %get-tuple-element.208, s32[64]{0:T(128)S(1)} %compare_select_fusion.4, f32[64,128,256]{2,1,0:T(8,128)} %broadcast_multiply_fusion.2), kind=kCustom, calls=%fused_computation.1.clone.1 | custom fusion | flops 2097152 | bytes 25166080 | tf_op jit(solution)/shard_map/while/body/eval_jaxpr/scatter-add | solution.py:34
  426.3 0.7 compare_and_fusion.2
  427.0 8.6 %gather_fusion = bf16[64,128,256]{2,1,0:T(8,128)(2,1)} fusion(bf16[256,128,256]{2,1,0:T(8,128)(2,1)} %get-tuple-element.223, s32[1024]{0:T(1024)S(1)} %pad_clamp_fusion.2), kind=kCustom, calls=%fused_computation.clone.1 | custom fusion | bytes 8388864 | tf_op jit(solution)/shard_map/while/body/eval_jaxpr/jit(_take)/gather | solution.py:30
  435.6 7.4 %broadcast_multiply_fusion.2 = f32[64,128,256]{2,1,0:T(8,128)} fusion(f32[64]{0:T(128)S(1)} %get-tuple-element.193, bf16[64,128,256]{2,1,0:T(8,128)(2,1)} %gather_fusion, pred[64]{0:T(512)(128)(4,1)S(1)} %get-tuple-element.195, bf16[256,128,128]{2,1,0:T(8,128)(2,1)} %get-tuple-element.221, s32[]{:T(128)S(6)} %select_n.49), kind=kOutput, calls=%fused_computation.2.clone.1 | convolution fusion | flops 541065216 | bytes 14680388 | tf_op jit(solution)/shard_map/while/body/eval_jaxpr/kij,kjf->kif/dot_general | solution.py:31
  443.0 0.1 compare_select_fusion.4
  443.1 19.5 %scatter_fusion = f32[64,128,256]{2,1,0:T(8,128)} fusion(f32[64,128,256]{2,1,0:T(8,128)} %get-tuple-element.208, s32[64]{0:T(128)S(1)} %compare_select_fusion.4, f32[64,128,256]{2,1,0:T(8,128)} %broadcast_multiply_fusion.2), kind=kCustom, calls=%fused_computation.1.clone.1 | custom fusion | flops 2097152 | bytes 25166080 | tf_op jit(solution)/shard_map/while/body/eval_jaxpr/scatter-add | solution.py:34
  462.6 0.7 compare_and_fusion.2
  463.3 8.6 %gather_fusion = bf16[64,128,256]{2,1,0:T(8,128)(2,1)} fusion(bf16[256,128,256]{2,1,0:T(8,128)(2,1)} %get-tuple-element.223, s32[1024]{0:T(1024)S(1)} %pad_clamp_fusion.2), kind=kCustom, calls=%fused_computation.clone.1 | custom fusion | bytes 8388864 | tf_op jit(solution)/shard_map/while/body/eval_jaxpr/jit(_take)/gather | solution.py:30
  471.9 7.4 %broadcast_multiply_fusion.2 = f32[64,128,256]{2,1,0:T(8,128)} fusion(f32[64]{0:T(128)S(1)} %get-tuple-element.193, bf16[64,128,256]{2,1,0:T(8,128)(2,1)} %gather_fusion, pred[64]{0:T(512)(128)(4,1)S(1)} %get-tuple-element.195, bf16[256,128,128]{2,1,0:T(8,128)(2,1)} %get-tuple-element.221, s32[]{:T(128)S(6)} %select_n.49), kind=kOutput, calls=%fused_computation.2.clone.1 | convolution fusion | flops 541065216 | bytes 14680388 | tf_op jit(solution)/shard_map/while/body/eval_jaxpr/kij,kjf->kif/dot_general | solution.py:31
  479.3 0.1 compare_select_fusion.4
  479.4 19.4 %scatter_fusion = f32[64,128,256]{2,1,0:T(8,128)} fusion(f32[64,128,256]{2,1,0:T(8,128)} %get-tuple-element.208, s32[64]{0:T(128)S(1)} %compare_select_fusion.4, f32[64,128,256]{2,1,0:T(8,128)} %broadcast_multiply_fusion.2), kind=kCustom, calls=%fused_computation.1.clone.1 | custom fusion | flops 2097152 | bytes 25166080 | tf_op jit(solution)/shard_map/while/body/eval_jaxpr/scatter-add | solution.py:34
  498.8 0.7 compare_and_fusion.2
  499.6 8.6 %gather_fusion = bf16[64,128,256]{2,1,0:T(8,128)(2,1)} fusion(bf16[256,128,256]{2,1,0:T(8,128)(2,1)} %get-tuple-element.223, s32[1024]{0:T(1024)S(1)} %pad_clamp_fusion.2), kind=kCustom, calls=%fused_computation.clone.1 | custom fusion | bytes 8388864 | tf_op jit(solution)/shard_map/while/body/eval_jaxpr/jit(_take)/gather | solution.py:30
  508.2 7.4 %broadcast_multiply_fusion.2 = f32[64,128,256]{2,1,0:T(8,128)} fusion(f32[64]{0:T(128)S(1)} %get-tuple-element.193, bf16[64,128,256]{2,1,0:T(8,128)(2,1)} %gather_fusion, pred[64]{0:T(512)(128)(4,1)S(1)} %get-tuple-element.195, bf16[256,128,128]{2,1,0:T(8,128)(2,1)} %get-tuple-element.221, s32[]{:T(128)S(6)} %select_n.49), kind=kOutput, calls=%fused_computation.2.clone.1 | convolution fusion | flops 541065216 | bytes 14680388 | tf_op jit(solution)/shard_map/while/body/eval_jaxpr/kij,kjf->kif/dot_general | solution.py:31
  515.6 0.1 compare_select_fusion.4
  515.6 19.5 %scatter_fusion = f32[64,128,256]{2,1,0:T(8,128)} fusion(f32[64,128,256]{2,1,0:T(8,128)} %get-tuple-element.208, s32[64]{0:T(128)S(1)} %compare_select_fusion.4, f32[64,128,256]{2,1,0:T(8,128)} %broadcast_multiply_fusion.2), kind=kCustom, calls=%fused_computation.1.clone.1 | custom fusion | flops 2097152 | bytes 25166080 | tf_op jit(solution)/shard_map/while/body/eval_jaxpr/scatter-add | solution.py:34
  535.1 5.9 convert_element_type.28
  541.1 0.0 all-reduce.2.cloned.1.call-update
  541.1 125.2 %all-reduce.2.cloned.1.call-done = bf16[8192,256]{1,0:T(8,128)(2,1)} async-done(((bf16[8192,256]{1,0:T(8,128)(2,1)}), bf16[8192,256]{1,0:T(8,128)(2,1)}) %all-reduce.2.cloned.1.call-update) | async-done | bytes 4194320 | tf_op jit(solution)/shard_map/psum | solution.py:41
  666.2 0.0 copy-done
  666.2 2.1 convolution_convert_fusion
  (4 shorter events, 0.0 us)
Async XLA Ops:
  6.5 659.7 %copy-start = (bf16[256,256]{1,0:T(8,128)(2,1)S(1)}, bf16[256,256]{1,0:T(8,128)(2,1)}, u32[]{:S(2)}) copy-start(bf16[256,256]{1,0:T(8,128)(2,1)} %param.13) | copy-start | bytes 393220
  13.3 372.4 %all-to-all-start = ((bf16[32,1024,256]{2,1,0:T(8,128)(2,1)}), bf16[32,1024,256]{2,1,0:T(8,128)(2,1)}, u32[]{:S(2)}, u32[]{:S(2)}) async-start(bf16[32,1024,256]{2,1,0:T(8,128)(2,1)} %stack.2), calls=%async_computation | async-start | bytes 33554432 | tf_op jit(solution)/shard_map/all_to_all | solution.py:17
  24.5 365.4 %copy-start.1 = (s32[1,1,256]{2,1,0:T(1,128)S(1)}, s32[1,1,256]{2,1,0:T(1,128)}, u32[]{:S(2)}) copy-start(s32[1,1,256]{2,1,0:T(1,128)} %param.11) | copy-start | bytes 3076
  24.5 365.4 %copy-start.2 = (s32[1,1,256]{2,1,0:T(1,128)S(1)}, s32[1,1,256]{2,1,0:T(1,128)}, u32[]{:S(2)}) copy-start(s32[1,1,256]{2,1,0:T(1,128)} %param.10) | copy-start | bytes 3076
  24.6 641.7 %all-reduce.2.cloned.1.call-start = ((), (), s32[]{:S(2)}) async-start(), calls=%async_computation.1 | async-start | bytes 8388608 | tf_op jit(solution)/shard_map/psum | solution.py:41
Sparse Core Ops, SparseCore 0:
  541.2 124.9 all-reduce.1
